TPU v7x, 32 devices: a whole 2x2x4 slice. The times are simulated.
32 devices in a mesh: cell: 16 (over z, x, core), gene: 2 (over y).
Axes of the slice: x: 2, y: 2, z: 4, core: 2. Of those that a mesh axis runs over, the one named last changes fastest.
Arguments:
- counts: bfloat16 [15360, 16384], P('cell', 'gene'), as said below
- w_factor: float32 [15360, 128], P('cell'), may hold values from 0.004 to 2, as said below
- h_factor: float32 [128, 16384], P('cell', 'gene'), may hold values from 0.03 to 0.3, as said below
Outputs:
- w_updated: float32 [15360, 128], P('cell')
- h_updated: float32 [128, 16384], P('cell', 'gene')
Inputs may be any that keep to these rules, and one draw needn't show every extreme that they name: `counts`: nonnegative whole numbers. `w_factor`: positive. `h_factor`: positive.
All inputs are finite; a program needn't handle non-finite values.
Results may differ from a plain program's by a relative error of at most 0.00092.
Values may be sent and summed in bfloat16 or wider, within the bound.
No kernel may reach another device: no remote copies, remote signals or barrier semaphores. Data moves between devices by JAX's collectives and lax.ppermute only.
A program may use at most 64 MiB of HBM per device.

v0:
```python
import jax
import jax.numpy as jnp
from jax import lax
from jax.sharding import PartitionSpec as P


def per_device(counts, w_factor, h_factor):
    own_rows = h_factor.shape[0]
    rank = w_factor.shape[1]
    w_copy = w_factor.astype(jnp.bfloat16)
    row_offset = lax.axis_index("cell") * own_rows
    counts_float = counts.astype(jnp.float32)
    columns = w_copy
    modeled = jnp.dot(
        columns,
        lax.all_gather(h_factor.astype(jnp.bfloat16), "cell", axis=0, tiled=True),
        preferred_element_type=jnp.float32,
    )
    quotient = (counts_float / modeled).astype(jnp.bfloat16)
    columns = w_copy
    numerator = lax.psum_scatter(
        lax.dot_general(
            columns, quotient, (((0,), (0,)), ((), ())), preferred_element_type=jnp.float32
        ),
        "cell",
        scatter_dimension=0,
        tiled=True,
    )
    w_totals = lax.psum(jnp.sum(w_factor, axis=0), "cell")
    own_totals = lax.dynamic_slice_in_dim(w_totals, row_offset, own_rows, 0)
    h_updated = h_factor * numerator / own_totals[:, None]
    h_new_copy = lax.all_gather(h_updated.astype(jnp.bfloat16), "cell", axis=0, tiled=True)
    modeled_again = jnp.dot(w_copy, h_new_copy, preferred_element_type=jnp.float32)
    quotient_again = (counts_float / modeled_again).astype(jnp.bfloat16)
    partial_w = lax.dot_general(
        quotient_again, h_new_copy, (((1,), (1,)), ((), ())), preferred_element_type=jnp.float32
    )
    partial_totals = jnp.sum(h_new_copy.astype(jnp.float32), axis=1)
    w_share = lax.psum_scatter(partial_w, "gene", scatter_dimension=1, tiled=True)
    h_totals = lax.psum(partial_totals, "gene")
    share_width = rank // lax.axis_size("gene")
    col_offset = lax.axis_index("gene") * share_width
    w_own = lax.dynamic_slice_in_dim(w_factor, col_offset, share_width, 1)
    totals_own = lax.dynamic_slice_in_dim(h_totals, col_offset, share_width, 0)
    w_part = w_own * w_share / totals_own[None, :]
    w_updated = lax.all_gather(w_part, "gene", axis=1, tiled=True)
    return (w_updated, h_updated)


def solution(mesh):
    in_specs = (P("cell", "gene"), P("cell", None), P("cell", "gene"))
    out_specs = (P("cell", None), P("cell", "gene"))
    return jax.shard_map(
        per_device, mesh=mesh, in_specs=in_specs, out_specs=out_specs, check_vma=False
    )
```

profile of v0, /device:TPU:0, one launch (start us, length us, event | category | flops | bytes accessed | tf_op | source)
XLA Modules:
  0.0 248.2 jit_solution(8995357598601707280)
XLA Ops:
  7.2 1.6 convert_element_type.23
  8.9 46.0 %all-gather.3.cloned.1.call-done = bf16[128,8192]{1,0:T(8,128)(2,1)} async-done(((bf16[8,8192]{1,0:T(8,128)(2,1)}), bf16[128,8192]{1,0:T(8,128)(2,1)}) %all-gather.3.cloned.1.call-update) | async-done | bytes 2097168 | tf_op jit(solution)/shard_map/all_gather | solution.py:16
  54.9 16.7 %fusion.4 = f32[128,8192]{0,1:T(8,128)} fusion(bf16[960,8192]{1,0:T(8,128)(2,1)} %param.3, bf16[128,8192]{1,0:T(8,128)(2,1)} %all-gather.3.cloned.1.call-done, f32[960,128]{1,0:T(8,128)} %param.4), kind=kOutput, calls=%fused_computation.5 | convolution fusion | flops 4050370560 | bytes 22511616 | tf_op jit(solution)/shard_map/dot_general | solution.py:22
  71.6 5.6 %copy.14 = f32[128,8192]{1,0:T(8,128)} copy(f32[128,8192]{0,1:T(8,128)} %fusion.4) | data formatting | bytes 8388608
  77.3 0.9 copy-done.2
  78.2 2.6 %copy.10 = f32[8,8192]{0,1:T(8,128)} copy(f32[8,8192]{1,0:T(8,128)S(1)} %copy-done.2) | data formatting | bytes 524288 | tf_op args[2]
  80.8 0.1 reduce_sum.18
  80.9 31.7 %psum.14 = f32[128]{0:T(128)S(1)} all-reduce(f32[128]{0:T(128)S(1)} %reduce_sum.18), channel_id=1, replica_groups=mesh['cell'=16,'gene'=2] {'cell'}, use_global_device_ids=true, to_apply=%region_2.0 | all-reduce | flops 128 | bytes 1024 | tf_op jit(solution)/shard_map/psum | solution.py:29
  112.7 36.1 %reduce-scatter.7.cloned.1.call-done = f32[8,8192]{1,0:T(8,128)} async-done(((f32[128,8192]{1,0:T(8,128)}), f32[8,8192]{1,0:T(8,128)}) %reduce-scatter.7.cloned.1.call-update) | async-done | bytes 262160
  148.7 3.5 %copy.15 = f32[8,8192]{0,1:T(8,128)} copy(f32[8,8192]{1,0:T(8,128)} %reduce-scatter.7.cloned.1.call-done) | data formatting | bytes 524288
  152.2 5.9 %fusion.14 = (bf16[8,8192]{0,1:T(8,128)(2,1)S(1)}, f32[8,8192]{0,1:T(8,128)}) fusion(f32[8]{0:T(128)S(1)} %dynamic_slice.10, f32[8,8192]{0,1:T(8,128)} %copy.10, f32[8,8192]{0,1:T(8,128)} %copy.15), kind=kLoop, calls=%fused_computation.14 | loop fusion | flops 196608 | bytes 917536 | tf_op jit(solution)/shard_map/convert_element_type | solution.py:32
  158.1 1.4 copy.11
  159.6 0.2 reduce-scatter.5.cloned.1.call-start
  159.8 40.4 %all-gather.5.cloned.1.call-done = bf16[128,8192]{1,0:T(8,128)(2,1)} async-done(((bf16[8,8192]{1,0:T(8,128)(2,1)}), bf16[128,8192]{1,0:T(8,128)(2,1)}) %all-gather.5.cloned.1.call-update) | async-done | bytes 2097168 | tf_op jit(solution)/shard_map/all_gather | solution.py:32
  200.2 17.3 %fusion.9 = f32[960,128]{0,1:T(8,128)} fusion(bf16[128,8192]{1,0:T(8,128)(2,1)} %all-gather.5.cloned.1.call-done, bf16[960,8192]{1,0:T(8,128)(2,1)} %param.3, f32[960,128]{1,0:T(8,128)S(1)} %copy-done.1), kind=kOutput, calls=%fused_computation.7 | convolution fusion | flops 4050247680 | bytes 18808832 | tf_op jit(solution)/shard_map/dot_general | solution.py:35
  217.5 0.2 constant_dynamic-slice_fusion
  217.7 0.2 copy.16
  217.9 3.7 %copy.13 = f32[8,8192]{1,0:T(8,128)} copy(f32[8,8192]{0,1:T(8,128)} %get-tuple-element.7) | data formatting | bytes 524288
  221.6 0.4 convert_reduce_fusion
  221.9 5.1 %psum.15 = f32[128]{0:T(128)S(1)} all-reduce(f32[128]{0:T(128)S(1)} %convert_reduce_fusion), channel_id=1, replica_groups=mesh['cell'=16,'gene'=2] {'gene'}, use_global_device_ids=true, to_apply=%region_5.0 | all-reduce | flops 128 | bytes 1024 | tf_op jit(solution)/shard_map/psum | solution.py:40
  227.1 4.0 %reduce-scatter.5.cloned.1.call-done = f32[960,64]{0,1:T(8,128)} async-done(((f32[960,128]{0,1:T(8,128)}), f32[960,64]{0,1:T(8,128)}) %reduce-scatter.5.cloned.1.call-update) | async-done | bytes 245776 | tf_op jit(solution)/shard_map/reduce_scatter | solution.py:39
  231.1 1.0 multiply_divide_fusion.1
  232.1 8.5 %all_gather.11 = f32[960,128]{0,1:T(8,128)S(1)} all-gather(f32[960,64]{0,1:T(8,128)S(1)} %multiply_divide_fusion.1), channel_id=1, replica_groups=mesh['cell'=16,'gene'=2] {'gene'}, dimensions={1}, use_global_device_ids=true | all-gather | bytes 737280 | tf_op jit(solution)/shard_map/all_gather | solution.py:46
  240.7 1.0 copy.12
  (14 shorter events, 0.3 us)
Async XLA Ops:
  7.2 47.8 %all-gather.3.cloned.1.call-start = ((), (), s32[]{:S(2)}) async-start(), calls=%async_computation.2 | async-start | bytes 2228224 | tf_op jit(solution)/shard_map/all_gather | solution.py:16
  8.9 139.9 %reduce-scatter.7.cloned.1.call-start = ((), (), s32[]{:S(2)}) async-start(), calls=%async_computation.5 | async-start | bytes 4456448
  77.2 0.9 copy-start.2
  77.3 3.5 %copy-start.1 = (f32[960,128]{1,0:T(8,128)S(1)}, f32[960,128]{1,0:T(8,128)}, u32[]{:S(2)}) copy-start(f32[960,128]{1,0:T(8,128)} %param.4) | copy-start | bytes 1474564
  77.3 122.9 %all-gather.5.cloned.1.call-start = ((), (), s32[]{:S(2)}) async-start(), calls=%async_computation.3 | async-start | bytes 2228224 | tf_op jit(solution)/shard_map/all_gather | solution.py:32
  159.6 71.5 %reduce-scatter.5.cloned.1.call-start = ((), (), s32[]{:S(2)}) async-start(), calls=%async_computation.4 | async-start | bytes 786432 | tf_op jit(solution)/shard_map/reduce_scatter | solution.py:39
  217.5 4.1 %copy-start = (bf16[128,8192]{1,0:T(8,128)(2,1)S(1)}, bf16[128,8192]{1,0:T(8,128)(2,1)}, u32[]{:S(2)}) copy-start(bf16[128,8192]{1,0:T(8,128)(2,1)} %all-gather.5.cloned.1.call-done) | copy-start | bytes 6291460
Sparse Core Ops, SparseCore 0:
  10.7 44.1 all-gather.2
  77.4 71.2 reduce-scatter.6
  159.7 40.4 all-gather.4
  217.6 13.4 reduce-scatter.4
where the time goes:
time: 249 us; the launch traced here: 248 us
  waiting for transfers between devices  126 us (51%)
  blocking collectives  45.4 us (18%)
  matrix products  34 us (14%)
  local copies, waits for them, and re-layouts  19.2 us (8%)
  between operations  13.8 us (6%)
  other arithmetic  9.09 us (4%)
    all_gather x1, waiting for transfers between devices, per_device(): lax.all_gather(h_factor.astype(jnp.bfloat16), 'cell', axis=0, tiled=True)  46 us
    all_gather x1, waiting for transfers between devices, per_device(): lax.all_gather(h_updated.astype(jnp.bfloat16), 'cell', axis=0, tiled=True)  40.4 us
    unnamed x5, waiting for transfers between devices  36.1 us
    psum x1, blocking collectives, per_device(): w_totals = lax.psum(jnp.sum(w_factor, axis=0), 'cell')  31.7 us
    unnamed x12, local copies, waits for them, and re-layouts  17.4 us
    dot_general x1, matrix products, per_device(): lax.dot_general(quotient_again, h_new_copy, (((1,), (1,)), ((), ())), pre...  17.3 us
    dot_general x1, matrix products, per_device(): lax.dot_general(columns, quotient, (((0,), (0,)), ((), ())), preferred_el...  16.7 us
    all_gather x1, blocking collectives, per_device(): w_updated = lax.all_gather(w_part, 'gene', axis=1, tiled=True)  8.55 us
  transfers between devices with their start and end apart: 4, of which 4 were waited for; matrix products, arithmetic and copies ran while one was open for 3% of the time, Pallas kernels for 0%

commit v1 on v0

--- a/solution.py
+++ b/solution.py
@@ -2,6 +2,23 @@
 import jax.numpy as jnp
 from jax import lax
 from jax.sharding import PartitionSpec as P
+
+
+def joined_along(pieces, dim):
+    pieces = jnp.moveaxis(pieces, 0, dim)
+    shape = pieces.shape
+    return pieces.reshape(*shape[:dim], shape[dim] * shape[dim + 1], *shape[dim + 2 :])
+
+
+def doubled(x, axis):
+    peers, index = (lax.axis_size(axis), lax.axis_index(axis))
+    tiles, bit = (x[None], 1)
+    while bit < peers:
+        other = lax.ppermute(tiles, axis, [(i, i ^ bit) for i in range(peers)])
+        low = index & bit == 0
+        tiles = jnp.concatenate([jnp.where(low, tiles, other), jnp.where(low, other, tiles)])
+        bit *= 2
+    return tiles
 
 
 def per_device(counts, w_factor, h_factor):
@@ -29,7 +46,8 @@
     w_totals = lax.psum(jnp.sum(w_factor, axis=0), "cell")
     own_totals = lax.dynamic_slice_in_dim(w_totals, row_offset, own_rows, 0)
     h_updated = h_factor * numerator / own_totals[:, None]
-    h_new_copy = lax.all_gather(h_updated.astype(jnp.bfloat16), "cell", axis=0, tiled=True)
+    x = h_updated.astype(jnp.bfloat16)
+    h_new_copy = joined_along(doubled(x, "cell"), 0)
     modeled_again = jnp.dot(w_copy, h_new_copy, preferred_element_type=jnp.float32)
     quotient_again = (counts_float / modeled_again).astype(jnp.bfloat16)
     partial_w = lax.dot_general(

time: 249 us -> 284 us (1.14)
  waiting for transfers between devices: 126 us -> 153 us
  other arithmetic: 9.09 us -> 14.6 us
  local copies, waits for them, and re-layouts: 19.2 us -> 23.8 us
  matrix products: 34 us -> 29.9 us
    ppermute x0 -> x4, waiting for transfers between devices: none -> 67.2 us  [doubled(): other = lax.ppermute(tiles, axis, [(i, i ^ bit) for i in range(peers)])]
    all_gather x1 -> x0, waiting for transfers between devices: 40.4 us -> none  [per_device(): lax.all_gather(h_updated.astype(jnp.bfloat16), 'cell', axis=0, tiled=True)]
    broadcast_in_dim x0 -> x1, other arithmetic: none -> 5.95 us  [doubled(): tiles, bit = (x[None], 1)]
    convert_element_type x1 -> x0, other arithmetic: 5.94 us -> none  [per_device(): h_updated.astype(jnp.bfloat16)]
    select_n x0 -> x4, other arithmetic: none -> 5.31 us  [doubled(): jnp.where(low, tiles, other)]
    dot_general x1, matrix products: 17.3 us -> 13.2 us  [per_device(): lax.dot_general(quotient_again, h_new_copy, (((1,), (1,)), ((), ())), pre...]
    select_n x0 -> x2, local copies, waits for them, and re-layouts: none -> 3.69 us  [the longest x1 1.85 us: doubled(): jnp.where(low, other, tiles)]
    ppermute x0 -> x4, starting transfers between devices: none -> 2.88 us  [doubled(): other = lax.ppermute(tiles, axis, [(i, i ^ bit) for i in range(peers)])]
  transfers between devices with their start and end apart: 4 -> 7, of which waited for: 4 -> 7; matrix products, arithmetic and copies ran while one was open for 3% -> 3% of each run, Pallas kernels for 0% -> 0%
where the time goes in v1:
time: 284 us
  waiting for transfers between devices  153 us (54%)
  blocking collectives  45.7 us (16%)
  matrix products  29.9 us (11%)
  local copies, waits for them, and re-layouts  23.8 us (8%)
  other arithmetic  14.6 us (5%)
  between operations  13.8 us (5%)
  starting transfers between devices  3.01 us (1%)
    ppermute x4, waiting for transfers between devices, doubled(): other = lax.ppermute(tiles, axis, [(i, i ^ bit) for i in range(peers)])  67.2 us
    all_gather x1, waiting for transfers between devices, per_device(): lax.all_gather(h_factor.astype(jnp.bfloat16), 'cell', axis=0, tiled=True)  46 us
    unnamed x4, waiting for transfers between devices  35.8 us
    psum x1, blocking collectives, per_device(): w_totals = lax.psum(jnp.sum(w_factor, axis=0), 'cell')  32 us
    unnamed x12, local copies, waits for them, and re-layouts  17.2 us
    dot_general x1, matrix products, per_device(): lax.dot_general(columns, quotient, (((0,), (0,)), ((), ())), preferred_el...  16.7 us
    dot_general x1, matrix products, per_device(): lax.dot_general(quotient_again, h_new_copy, (((1,), (1,)), ((), ())), pre...  13.2 us
    all_gather x1, blocking collectives, per_device(): w_updated = lax.all_gather(w_part, 'gene', axis=1, tiled=True)  8.55 us
  transfers between devices with their start and end apart: 7, of which 7 were waited for; matrix products, arithmetic and copies ran while one was open for 3% of the time, Pallas kernels for 0%

profile of v1, /device:TPU:0, one launch (start us, length us, event | category | flops | bytes accessed | tf_op | source)
XLA Modules:
  0.0 283.9 jit_solution(13033812407531663100)
XLA Ops:
  7.2 1.6 convert_element_type.24
  8.9 46.0 %all-gather.2.cloned.1.call-done = bf16[128,8192]{1,0:T(8,128)(2,1)} async-done(((bf16[8,8192]{1,0:T(8,128)(2,1)}), bf16[128,8192]{1,0:T(8,128)(2,1)}) %all-gather.2.cloned.1.call-update) | async-done | bytes 2097168 | tf_op jit(solution)/shard_map/all_gather | solution.py:33
  54.9 16.7 %fusion.4 = f32[128,8192]{0,1:T(8,128)} fusion(bf16[960,8192]{1,0:T(8,128)(2,1)} %param.3, bf16[128,8192]{1,0:T(8,128)(2,1)} %all-gather.2.cloned.1.call-done, f32[960,128]{1,0:T(8,128)} %param.4), kind=kOutput, calls=%fused_computation.5 | convolution fusion | flops 4050370560 | bytes 22511616 | tf_op jit(solution)/shard_map/dot_general | solution.py:39
  71.6 5.6 %copy.23 = f32[128,8192]{1,0:T(8,128)} copy(f32[128,8192]{0,1:T(8,128)} %fusion.4) | data formatting | bytes 8388608
  78.1 2.6 copy.15
  80.9 32.0 %psum.14 = f32[128]{0:T(128)S(1)} all-reduce(f32[128]{0:T(128)S(1)} %reduce_sum.20), channel_id=1, replica_groups=mesh['cell'=16,'gene'=2] {'cell'}, use_global_device_ids=true, to_apply=%region_2.0 | all-reduce | flops 128 | bytes 1024 | tf_op jit(solution)/shard_map/psum | solution.py:46
  112.9 35.8 %reduce-scatter.7.cloned.1.call-done = f32[8,8192]{1,0:T(8,128)} async-done(((f32[128,8192]{1,0:T(8,128)}), f32[8,8192]{1,0:T(8,128)}) %reduce-scatter.7.cloned.1.call-update) | async-done | bytes 262160
  148.7 3.5 %copy.24 = f32[8,8192]{0,1:T(8,128)} copy(f32[8,8192]{1,0:T(8,128)} %reduce-scatter.7.cloned.1.call-done) | data formatting | bytes 524288
  152.2 6.0 %convert_bitcast_fusion = (bf16[1,8,8192]{1,2,0:T(8,128)(2,1)S(1)}, f32[8,8192]{0,1:T(8,128)}) fusion(f32[8]{0:T(128)S(1)} %dynamic_slice.10, f32[8,8192]{0,1:T(8,128)} %copy.15, f32[8,8192]{0,1:T(8,128)} %copy.24), kind=kLoop, calls=%fused_computation.12 | loop fusion | flops 196608 | bytes 917536 | tf_op jit(solution)/shard_map/broadcast_in_dim | solution.py:15
  159.0 1.3 collective-permute-done
  160.3 1.7 copy.17
  162.0 3.8 %broadcast_select_fusion.1 = (bf16[1,8,8192]{1,2,0:T(8,128)(2,1)}, bf16[1,8,8192]{1,2,0:T(8,128)(2,1)}) fusion(bf16[1,8,8192]{1,2,0:T(8,128)(2,1)S(1)} %get-tuple-element.8, bf16[1,8,8192]{1,2,0:T(8,128)(2,1)} %copy.17, pred[]{:T(512)S(6)} %eq.15), kind=kLoop, calls=%fused_computation.14 | loop fusion | flops 131072 | bytes 524289 | tf_op jit(solution)/shard_map/jit(_where)/select_n | solution.py:19
  165.8 1.8 copy.19
  167.7 1.9 copy.20
  170.1 7.9 %collective-permute-done.1 = bf16[2,8,8192]{2,1,0:T(8,128)(2,1)S(1)} collective-permute-done((bf16[2,8,8192]{2,1,0:T(8,128)(2,1)S(1)}, bf16[2,8,8192]{2,1,0:T(8,128)(2,1)S(1)}, u32[]{:S(2)}, u32[]{:S(2)}) %collective-permute-start.1) | collective-permute-done | bytes 262176 | tf_op jit(solution)/shard_map/ppermute | solution.py:17
  179.1 12.2 %collective-permute-done.2 = bf16[4,8,8192]{2,1,0:T(8,128)(2,1)S(1)} collective-permute-done((bf16[4,8,8192]{2,1,0:T(8,128)(2,1)S(1)}, bf16[4,8,8192]{2,1,0:T(8,128)(2,1)S(1)}, u32[]{:S(2)}, u32[]{:S(2)}) %collective-permute-start.2) | collective-permute-done | bytes 524320 | tf_op jit(solution)/shard_map/ppermute | solution.py:17
  191.5 1.3 collective-permute-start.3
  192.8 45.7 %collective-permute-done.3 = bf16[8,8,8192]{2,1,0:T(8,128)(2,1)} collective-permute-done((bf16[8,8,8192]{2,1,0:T(8,128)(2,1)S(1)}, bf16[8,8,8192]{2,1,0:T(8,128)(2,1)}, u32[]{:S(2)}, u32[]{:S(2)}) %collective-permute-start.3) | collective-permute-done | bytes 1048608 | tf_op jit(solution)/shard_map/ppermute | solution.py:17
  238.5 1.4 broadcast_select_fusion.3
  239.9 13.2 %fusion.9 = f32[960,128]{0,1:T(8,128)} fusion(bf16[960,8192]{1,0:T(8,128)(2,1)} %param.3, bf16[8,8,8192]{2,1,0:T(8,128)(2,1)S(1)} %get-tuple-element.13, bf16[8,8,8192]{2,1,0:T(8,128)(2,1)S(1)} %get-tuple-element.12, f32[960,128]{1,0:T(8,128)} %param.4), kind=kOutput, calls=%fused_computation.7 | convolution fusion | flops 4052344832 | bytes 18808832 | tf_op jit(solution)/shard_map/dot_general | solution.py:53
  253.5 3.5 %copy.22 = f32[8,8192]{1,0:T(8,128)} copy(f32[8,8192]{0,1:T(8,128)} %get-tuple-element.9) | data formatting | bytes 524288
  257.5 5.1 %psum.15 = f32[128]{0:T(128)S(1)} all-reduce(f32[128]{0:T(128)S(1)} %reduce_sum.22), channel_id=1, replica_groups=mesh['cell'=16,'gene'=2] {'gene'}, use_global_device_ids=true, to_apply=%region_5.6 | all-reduce | flops 128 | bytes 1024 | tf_op jit(solution)/shard_map/psum | solution.py:58
  262.7 4.1 %reduce-scatter.5.cloned.1.call-done = f32[960,64]{0,1:T(8,128)} async-done(((f32[960,128]{0,1:T(8,128)}), f32[960,64]{0,1:T(8,128)}) %reduce-scatter.5.cloned.1.call-update) | async-done | bytes 245776 | tf_op jit(solution)/shard_map/reduce_scatter | solution.py:57
  267.9 8.6 %all_gather.7 = f32[960,128]{0,1:T(8,128)S(1)} all-gather(f32[960,64]{0,1:T(8,128)S(1)} %multiply_divide_fusion.1), channel_id=1, replica_groups=mesh['cell'=16,'gene'=2] {'gene'}, dimensions={1}, use_global_device_ids=true | all-gather | bytes 737280 | tf_op jit(solution)/shard_map/all_gather | solution.py:64
  (30 shorter events, 6.8 us)
Async XLA Ops:
  7.2 47.8 %all-gather.2.cloned.1.call-start = ((), (), s32[]{:S(2)}) async-start(), calls=%async_computation.2 | async-start | bytes 2228224 | tf_op jit(solution)/shard_map/all_gather | solution.py:33
  8.9 139.8 %reduce-scatter.7.cloned.1.call-start = ((), (), s32[]{:S(2)}) async-start(), calls=%async_computation.4 | async-start | bytes 4456448
  77.2 0.9 copy-start.2
  77.2 3.5 %copy-start = (f32[960,128]{1,0:T(8,128)S(1)}, f32[960,128]{1,0:T(8,128)}, u32[]{:S(2)}) copy-start(f32[960,128]{1,0:T(8,128)} %param.4) | copy-start | bytes 1474564
  77.2 189.6 %reduce-scatter.5.cloned.1.call-start = ((), (), s32[]{:S(2)}) async-start(), calls=%async_computation.3 | async-start | bytes 786432 | tf_op jit(solution)/shard_map/reduce_scatter | solution.py:57
  158.9 1.4 collective-permute-start
  169.6 8.4 %collective-permute-start.1 = (bf16[2,8,8192]{2,1,0:T(8,128)(2,1)S(1)}, bf16[2,8,8192]{2,1,0:T(8,128)(2,1)S(1)}, u32[]{:S(2)}, u32[]{:S(2)}) collective-permute-start(bf16[2,8,8192]{2,1,0:T(8,128)(2,1)S(1)} %pad_maximum_fusion.5), channel_id=1, source_target_pairs={{0,4},{2,6},{4,0},{6,2},{8,12},{10,14},{12,8},{14,10},{16,20},{18,... | collective-permute-start | bytes 786440 | tf_op jit(solution)/shard_map/ppermute | solution.py:17
  178.1 13.2 %collective-permute-start.2 = (bf16[4,8,8192]{2,1,0:T(8,128)(2,1)S(1)}, bf16[4,8,8192]{2,1,0:T(8,128)(2,1)S(1)}, u32[]{:S(2)}, u32[]{:S(2)}) collective-permute-start(bf16[4,8,8192]{2,1,0:T(8,128)(2,1)S(1)} %pad_maximum_fusion.4), channel_id=1, source_target_pairs={{0,8},{2,10},{4,12},{6,14},{8,0},{10,2},{12,4},{14,6},{16,24},{18,... | collective-permute-start | bytes 1572872 | tf_op jit(solution)/shard_map/ppermute | solution.py:17
  191.5 47.0 %collective-permute-start.3 = (bf16[8,8,8192]{2,1,0:T(8,128)(2,1)S(1)}, bf16[8,8,8192]{2,1,0:T(8,128)(2,1)}, u32[]{:S(2)}, u32[]{:S(2)}) collective-permute-start(bf16[8,8,8192]{2,1,0:T(8,128)(2,1)S(1)} %pad_maximum_fusion.3), channel_id=1, source_target_pairs={{0,16},{2,18},{4,20},{6,22},{8,24},{10,26},{12,28},{14,30},{16,0},... | collective-permute-start | bytes 3145736 | tf_op jit(solution)/shard_map/ppermute | solution.py:17
  239.9 13.3 %copy-start.1 = (f32[960,128]{1,0:T(8,128)S(1)}, f32[960,128]{1,0:T(8,128)}, u32[]{:S(2)}) copy-start(f32[960,128]{1,0:T(8,128)} %param.4) | copy-start | bytes 1474564
Sparse Core Ops, SparseCore 0:
  10.7 44.1 all-gather.1
  77.3 71.2 reduce-scatter.6
  253.3 13.5 reduce-scatter.4
